TPU v7x, 512 devices: a whole 4x8x8 slice. The times are simulated.
512 devices in a mesh: grp: 2 (over core), blk: 128 (over z_lo, y, x), real: 2 (over z_hi).
Axes of the slice: x: 4, y: 8, z: 8 (z_hi: 2, z_lo: 4; z = z_hi * 4 + z_lo), core: 2. Of those that a mesh axis runs over, the one named last changes fastest.
Arguments:
- sky_data: float32 [32, 256, 8192], P('real', 'blk', 'grp'), may hold values from -6 to 6
- signal_prev: float32 [32, 256, 8192], P('real', 'blk', 'grp'), may hold values from -6 to 6
- noise_var: float32 [256, 8192], P('blk', 'grp'), may hold values from 1 to 16
- mask_flags: int32 [256, 8192], P('blk', 'grp'), may hold values 0 or 1
- cycle_table: int32 [256], P('blk'), may hold values from 0 to 255, each once
- m_table: int32 [512], replicated, may hold values from 0 to 4095, as said below
- spectrum: float32 [4096], P(('grp', 'real')), may hold values from 0.05 to 5
- legendre: bfloat16 [512, 4096, 256], P('blk', ('grp', 'real')), may hold values from -0.375 to 0.375
Outputs:
- wiener_alm: float32 [32, 2, 512, 4096], P(None, None, 'blk', ('grp', 'real'))
- signal_next: float32 [32, 256, 8192], P('real', 'blk', 'grp')
Inputs may be any that keep to these rules, and one draw needn't show every extreme that they name: `m_table`: distinct orders; 0 and 4095 are always among them. `cycle_table`: each cycle number once.
All inputs are finite; a program needn't handle non-finite values. No bound on the sum of `mask_flags` on one device may be relied on, other than what follows from the above.
Results may differ from a plain program's by a relative error of at most 0.0063.
Values may be sent and summed in bfloat16 or wider, within the bound.
A program may use at most 64 MiB of HBM per device.

v0:
```python
import math

import jax
import jax.numpy as jnp
from jax import lax
from jax.sharding import PartitionSpec as P


def copy_for_each(x, axis):
    peers = lax.axis_size(axis)
    return lax.all_to_all(jnp.broadcast_to(x[None], (peers, *x.shape)), axis, 0, 0, tiled=True)


def of_everyone(x, axis):
    everything = copy_for_each(x, axis)
    return jnp.sum(everything, axis=0)


def in_one(arrays, axis):
    ends = [0]
    for a in arrays:
        ends.append(ends[-1] + a.size)
    subtotal = of_everyone(jnp.concatenate([a.ravel() for a in arrays]), axis)
    return tuple((subtotal[b:e].reshape(a.shape) for a, b, e in zip(arrays, ends, ends[1:])))


def side_by_side(arrays, axis, split_dim, concat_dim, along):
    both = jnp.concatenate(arrays, axis=along)
    whole, at, finished = (
        lax.all_to_all(both, axis, split_axis=split_dim, concat_axis=concat_dim, tiled=True),
        0,
        [],
    )
    for a in arrays:
        finished.append(lax.slice_in_dim(whole, at, at + a.shape[along], axis=along))
        at += a.shape[along]
    return tuple(finished)


def in_one_piece(arrays, axis, dim, along):
    both = jnp.concatenate(arrays, axis=along)
    whole, at, finished = (lax.all_gather(both, axis, axis=dim, tiled=True), 0, [])
    for a in arrays:
        finished.append(lax.slice_in_dim(whole, at, at + a.shape[along], axis=along))
        at += a.shape[along]
    return tuple(finished)


def split_up(x, dim, peers):
    before, after = (x.shape[:dim], x.shape[dim + 1 :])
    return jnp.moveaxis(x.reshape(*before, peers, -1, *after), dim, 0)


def sum_at_owner(x, axis, dim):
    parts = split_up(x, dim, lax.axis_size(axis))
    arrived = lax.all_to_all(parts, axis, split_axis=0, concat_axis=0, tiled=True)
    return arrived.sum(axis=0)


def unit_circle(col_ids, mode_ids, cycle_len):
    product_ids = col_ids[:, None] * mode_ids[None, :] % cycle_len
    angles = product_ids.astype(jnp.float32) * (2.0 * math.pi / cycle_len)
    return jnp.cos(angles), jnp.sin(angles)


def phase_tables(first_col, half_len, mode_ids, cycle_len):
    fine_count = 64
    coarse_count = half_len // fine_count
    coarse_cols = first_col + fine_count * jnp.arange(coarse_count, dtype=jnp.int32)
    coarse_cos, coarse_sin = unit_circle(coarse_cols, mode_ids, cycle_len)
    fine_cos, fine_sin = unit_circle(
        jnp.arange(fine_count, dtype=jnp.int32), mode_ids, cycle_len
    )
    coarse_cos, coarse_sin, fine_cos, fine_sin = lax.optimization_barrier(
        (coarse_cos, coarse_sin, fine_cos, fine_sin)
    )
    a, b = coarse_cos[:, None], coarse_sin[:, None]
    c, d = fine_cos[None], fine_sin[None]
    cos_tab = (a * c - b * d).astype(jnp.bfloat16).reshape(half_len, -1)
    sin_tab = (b * c + a * d).astype(jnp.bfloat16).reshape(half_len, -1)
    return lax.optimization_barrier((cos_tab, sin_tab))


def cycle_offsets(cycle_ids, mode_ids, cycle_len):
    parity = (cycle_ids % 2).astype(jnp.float32)
    shifts = math.pi / cycle_len * parity[:, None] * mode_ids[None, :].astype(jnp.float32)
    return (jnp.cos(shifts), jnp.sin(shifts))


def forward_modes(re_part, im_part):
    summed = in_one((re_part, im_part), "grp")
    fourier_pair = (summed[0].astype(jnp.bfloat16), summed[1].astype(jnp.bfloat16))
    fourier_pair = side_by_side((fourier_pair[0], fourier_pair[1]), "blk", 2, 1, 0)
    fourier_pair = in_one_piece((fourier_pair[0], fourier_pair[1]), "real", 0, 1)
    return fourier_pair


def backward_cycles(partial_value):
    summed = sum_at_owner(partial_value, "real", 0)
    reduced = of_everyone(summed, "grp")
    cycle_pair = lax.all_to_all(
        reduced.astype(jnp.bfloat16), "blk", split_axis=2, concat_axis=3, tiled=True
    )
    return cycle_pair


def per_device(
    sky_data, signal_prev, noise_var, mask_flags, cycle_table, m_table, spectrum, legendre
):
    real_dev, cycle_dev, half_len = sky_data.shape
    cycle_len = half_len * lax.axis_size("grp")
    mode_count = m_table.shape[0]
    first_col = lax.axis_index("grp") * half_len
    cos_tab, sin_tab = phase_tables(first_col, half_len, m_table, cycle_len)
    cos_shift, sin_shift = cycle_offsets(cycle_table, m_table, cycle_len)
    weight = mask_flags.astype(jnp.float32) / (noise_var - 0.5)
    messenger = (weight * sky_data + 2.0 * signal_prev) / (weight + 2.0)
    flat_rows = messenger.astype(jnp.bfloat16).reshape(real_dev * cycle_dev, half_len)
    base_cos = jnp.dot(flat_rows, cos_tab, preferred_element_type=jnp.float32).reshape(
        real_dev, cycle_dev, mode_count
    )
    base_sin = -jnp.dot(flat_rows, sin_tab, preferred_element_type=jnp.float32).reshape(
        real_dev, cycle_dev, mode_count
    )
    norm_scale = cycle_len ** (-0.5)
    re_part = (base_cos * cos_shift + base_sin * sin_shift) * norm_scale
    im_part = (base_sin * cos_shift - base_cos * sin_shift) * norm_scale
    fourier_re, fourier_im = forward_modes(re_part, im_part)
    fourier = jnp.stack([fourier_re, fourier_im], 1)
    coefficients = jnp.einsum(
        "mlr,kcrm->kcml", legendre, fourier, preferred_element_type=jnp.float32
    )
    factor = spectrum / (spectrum + 0.5)
    wiener_alm = coefficients * factor
    total_l = legendre.shape[1] * lax.axis_size("grp") * lax.axis_size("real")
    syn_scale = (legendre.shape[2] / total_l) ** 0.5
    partial_value = (
        jnp.einsum(
            "mlr,kcml->kcrm",
            legendre,
            wiener_alm.astype(jnp.bfloat16),
            preferred_element_type=jnp.float32,
        )
        * syn_scale
    )
    cycle_pair = backward_cycles(partial_value)
    cycle_modes = cycle_pair.astype(jnp.float32)
    modes_re = cycle_modes[:, 0]
    modes_im = cycle_modes[:, 1]
    rotated_re = (modes_re * cos_shift - modes_im * sin_shift).astype(jnp.bfloat16)
    rotated_im = (modes_im * cos_shift + modes_re * sin_shift).astype(jnp.bfloat16)
    contract = (((1,), (1,)), ((), ()))
    pixel_sum = lax.dot_general(
        rotated_re.reshape(-1, mode_count), cos_tab, contract, preferred_element_type=jnp.float32
    )
    pixel_sum = pixel_sum - lax.dot_general(
        rotated_im.reshape(-1, mode_count), sin_tab, contract, preferred_element_type=jnp.float32
    )
    signal_next = (pixel_sum * mode_count ** (-0.5)).reshape(real_dev, cycle_dev, half_len)
    return (wiener_alm, signal_next)


def solution(mesh):
    in_specs = (
        P("real", "blk", "grp"),
        P("real", "blk", "grp"),
        P("blk", "grp"),
        P("blk", "grp"),
        P("blk"),
        P(),
        P(("grp", "real")),
        P("blk", ("grp", "real"), None),
    )
    out_specs = (P(None, None, "blk", ("grp", "real")), P("real", "blk", "grp"))
    return jax.shard_map(
        per_device, mesh=mesh, in_specs=in_specs, out_specs=out_specs, check_vma=False
    )
```

profile of v0, /device:TPU:1, one launch (start us, length us, event | category | flops | bytes accessed | tf_op | source)
XLA Modules:
  0.0 107.0 jit_solution(4546864259246799511)
XLA Ops:
  0.7 0.8 convert_element_type.76
  1.5 1.7 %fusion.39 = (f32[64,512]{1,0:T(8,128)S(1)}, f32[64,512]{1,0:T(8,128)S(1)}, f32[64,512]{1,0:T(8,128)S(1)}, f32[64,512]{1,0:T(8,128)S(1)}) fusion(s32[512]{0:T(512)} %param.13, s32[64]{0:T(128)S(1)} %multiply_add_fusion), kind=kLoop, calls=%fused_computation.54 | loop fusion | flops 917504 | bytes 526592 | tf_op jit(solution)/shard_map/sin | solution.py:63
  3.3 3.2 %add_convert_fusion = (bf16[64,64,512]{2,1,0:T(8,128)(2,1)S(1)}, bf16[64,64,512]{2,1,0:T(8,128)(2,1)S(1)}) fusion(f32[64,512]{1,0:T(8,128)S(1)} %get-tuple-element.11, f32[64,512]{1,0:T(8,128)S(1)} %get-tuple-element.10, f32[64,512]{1,0:T(8,128)S(1)} %get-tuple-element.9, f32[64,512]{1,0:T(8,128)S(1)} %get-tuple-element.8), kind=kLoop, calls=%fused_computation | loop fusion | flops 16777216 | bytes 8912896 | tf_op jit(solution)/shard_map/convert_element_type | solution.py:80
  7.0 0.9 fusion.3
  8.0 0.9 add_multiply_fusion
  8.9 0.8 copy-done.3
  10.0 10.4 %all_to_all.40 = f32[2,1,32768]{2,1,0:T(1,128)S(1)} all-to-all(f32[2,1,32768]{2,1,0:T(1,128)S(1)} %broadcast_in_dim.4), channel_id=1, replica_groups=mesh['grp'=2,'blk'=128,'real'=2] {'grp'}, dimensions={0} | all-to-all | bytes 524288 | tf_op jit(solution)/shard_map/all_to_all | solution.py:11
  21.2 0.8 reshape.159
  22.0 11.6 %all-to-all-start.1 = ((bf16[128,2,128]{2,1,0:T(2,128)(2,1)}), bf16[128,2,128]{2,1,0:T(2,128)(2,1)S(1)}, u32[]{:S(2)}, u32[]{:S(2)}) async-start(bf16[128,2,128]{2,1,0:T(2,128)(2,1)} %reshape.159), calls=%async_computation.1 | async-start | bytes 131072 | tf_op jit(solution)/shard_map/all_to_all | solution.py:30
  33.7 11.1 %all-to-all-done.1 = bf16[128,2,128]{2,1,0:T(2,128)(2,1)S(1)} async-done(((bf16[128,2,128]{2,1,0:T(2,128)(2,1)}), bf16[128,2,128]{2,1,0:T(2,128)(2,1)S(1)}, u32[]{:S(2)}, u32[]{:S(2)}) %all-to-all-start.1) | async-done | bytes 65568 | tf_op jit(solution)/shard_map/all_to_all | solution.py:30
  46.0 8.6 %all_gather.3 = bf16[32,512,4]{1,0,2:T(8,128)(2,1)S(1)} all-gather(bf16[16,512,4]{1,0,2:T(8,128)(2,1)S(1)} %pad_maximum_fusion.2), channel_id=1, replica_groups=mesh['grp'=2,'blk'=128,'real'=2] {'real'}, dimensions={0}, use_global_device_ids=true | all-gather | bytes 196608 | tf_op jit(solution)/shard_map/all_gather | solution.py:42
  54.7 0.8 fusion.12
  55.4 0.5 fusion.15
  55.9 16.3 %all_to_all.41 = f32[2,16,2,256,4]{3,1,2,4,0:T(8,128)S(1)} all-to-all(f32[2,16,2,256,4]{3,1,2,4,0:T(8,128)S(1)} %copy.142), channel_id=1, replica_groups=mesh['grp'=2,'blk'=128,'real'=2] {'real'}, dimensions={0} | all-to-all | bytes 524288 | tf_op jit(solution)/shard_map/all_to_all | solution.py:56
  72.3 5.7 %all_to_all.42 = f32[2,16,2,256,4]{3,1,4,2,0:T(8,128)S(1)} all-to-all(f32[2,16,2,256,4]{3,1,4,2,0:T(8,128)S(1)} %broadcast_in_dim.5), channel_id=1, replica_groups=mesh['grp'=2,'blk'=128,'real'=2] {'grp'}, dimensions={0} | all-to-all | bytes 524288 | tf_op jit(solution)/shard_map/all_to_all | solution.py:11
  78.0 1.1 %copy.145 = bf16[16,2,256,4]{0,3,1,2:T(4,128)(2,1)} copy(bf16[16,2,256,4]{2,0,3,1:T(8,128)(2,1)S(1)} %reduce_sum.29) | data formatting | bytes 131072 | tf_op jit(solution)/shard_map/convert_element_type | solution.py:102
  79.1 2.0 %reshape.161 = bf16[128,2,128]{2,1,0:T(2,128)(2,1)} reshape(bf16[256,2,4,16]{3,2,1,0:T(4,128)(2,1)} %bitcast.68) | data formatting | bytes 131072
  81.2 6.4 %all-to-all-start.4 = ((bf16[128,2,128]{2,1,0:T(2,128)(2,1)}), bf16[128,2,128]{2,1,0:T(2,128)(2,1)S(1)}, u32[]{:S(2)}, u32[]{:S(2)}) async-start(bf16[128,2,128]{2,1,0:T(2,128)(2,1)} %reshape.161), calls=%async_computation.4 | async-start | bytes 131072 | tf_op jit(solution)/shard_map/all_to_all | solution.py:101
  87.7 1.6 %copy.153 = f32[32,2,4,1024]{3,2,1,0:T(4,128)} copy(f32[32,2,4,1024]{3,0,1,2:T(8,128)S(1)} %fusion.12) | data formatting | bytes 2097152
  89.4 9.4 %all-to-all-done.4 = bf16[128,2,128]{2,1,0:T(2,128)(2,1)S(1)} async-done(((bf16[128,2,128]{2,1,0:T(2,128)(2,1)}), bf16[128,2,128]{2,1,0:T(2,128)(2,1)S(1)}, u32[]{:S(2)}, u32[]{:S(2)}) %all-to-all-start.4) | async-done | bytes 65568 | tf_op jit(solution)/shard_map/all_to_all | solution.py:101
  99.6 0.7 copy.148
  100.9 3.6 %fusion.41 = f32[32,4096]{1,0:T(8,128)S(1)} fusion(bf16[4096,512]{1,0:T(8,128)(2,1)} %bitcast.64, f32[32,512]{1,0:T(8,128)S(1)} %squeeze.7, f32[32,512]{1,0:T(8,128)S(1)} %mul.267, f32[32,512]{1,0:T(8,128)S(1)} %squeeze.6, f32[32,512]{1,0:T(8,128)S(1)} %mul.265), kind=kOutput, calls=%fused_computation.56 | convolution fusion | flops 134283264 | bytes 4980736 | tf_op jit(solution)/shard_map/dot_general | solution.py:153
  104.5 1.3 %fusion = f32[32,4096]{1,0:T(8,128)S(1)} fusion(f32[32,4096]{1,0:T(8,128)S(1)} %fusion.41, bf16[4096,512]{1,0:T(8,128)(2,1)S(1)} %bitcast.62, f32[32,512]{1,0:T(8,128)S(1)} %squeeze.6, f32[32,512]{1,0:T(8,128)S(1)} %mul.267, f32[32,512]{1,0:T(8,128)S(1)} %squeeze.7, f32[32,512]{1,0:T(8,128)S(1)} %mul.265), kind=kOutput, calls=%fused_computation.3 | convolution fusion | flops 134545408 | bytes 5505024 | tf_op jit(solution)/shard_map/dot_general | solution.py:156
  105.9 1.1 %reshape.153 = f32[16,2,4096]{2,1,0:T(2,128)} reshape(f32[32,4096]{1,0:T(8,128)S(1)} %fusion) | data formatting | bytes 1048576 | tf_op jit(solution)/shard_map/reshape | solution.py:159
  (62 shorter events, 4.6 us)
Async XLA Ops:
  0.6 54.0 %copy-start = (bf16[4,1024,256]{2,1,0:T(8,128)(2,1)S(1)}, bf16[4,1024,256]{2,1,0:T(8,128)(2,1)}, u32[]{:S(2)}) copy-start(bf16[4,1024,256]{2,1,0:T(8,128)(2,1)} %param.15) | copy-start | bytes 6291460
  3.2 3.3 %copy-start.9 = (s32[2]{0:T(128)S(1)}, s32[2]{0:T(128)}, u32[]{:S(2)}) copy-start(s32[2]{0:T(128)} %param.12) | copy-start | bytes 28
  3.2 3.3 %copy-start.6 = (f32[2,4096]{1,0:T(2,128)S(1)}, f32[2,4096]{1,0:T(2,128)}, u32[]{:S(2)}) copy-start(f32[2,4096]{1,0:T(2,128)} %param.10) | copy-start | bytes 98308
  3.3 3.3 %copy-start.7 = (s32[2,4096]{1,0:T(2,128)S(1)}, s32[2,4096]{1,0:T(2,128)}, u32[]{:S(2)}) copy-start(s32[2,4096]{1,0:T(2,128)} %param.11) | copy-start | bytes 98308
  3.3 3.3 %copy-start.4 = (f32[16,2,4096]{2,1,0:T(2,128)S(1)}, f32[16,2,4096]{2,1,0:T(2,128)}, u32[]{:S(2)}) copy-start(f32[16,2,4096]{2,1,0:T(2,128)} %param.9) | copy-start | bytes 1572868
  3.3 3.3 %copy-start.5 = (f32[16,2,4096]{2,1,0:T(2,128)S(1)}, f32[16,2,4096]{2,1,0:T(2,128)}, u32[]{:S(2)}) copy-start(f32[16,2,4096]{2,1,0:T(2,128)} %param.8) | copy-start | bytes 1572868
  6.5 2.4 %copy-start.1 = (bf16[64,64,512]{2,1,0:T(8,128)(2,1)}, bf16[64,64,512]{2,1,0:T(8,128)(2,1)S(1)}, u32[]{:S(2)}) copy-start(bf16[64,64,512]{2,1,0:T(8,128)(2,1)S(1)} %get-tuple-element.34) | copy-start | bytes 12582916
  6.5 3.2 %copy-start.3 = (bf16[64,64,512]{2,1,0:T(8,128)(2,1)}, bf16[64,64,512]{2,1,0:T(8,128)(2,1)S(1)}, u32[]{:S(2)}) copy-start(bf16[64,64,512]{2,1,0:T(8,128)(2,1)S(1)} %get-tuple-element.35) | copy-start | bytes 12582916
  8.0 25.6 %copy-start.8 = (f32[1024]{0:T(1024)S(1)}, f32[1024]{0:T(1024)}, u32[]{:S(2)}) copy-start(f32[1024]{0:T(1024)} %param.14) | copy-start | bytes 12292
  22.0 22.7 %all-to-all-start.1 = ((bf16[128,2,128]{2,1,0:T(2,128)(2,1)}), bf16[128,2,128]{2,1,0:T(2,128)(2,1)S(1)}, u32[]{:S(2)}, u32[]{:S(2)}) async-start(bf16[128,2,128]{2,1,0:T(2,128)(2,1)} %reshape.159), calls=%async_computation.1 | async-start | bytes 131072 | tf_op jit(solution)/shard_map/all_to_all | solution.py:30
  81.2 17.6 %all-to-all-start.4 = ((bf16[128,2,128]{2,1,0:T(2,128)(2,1)}), bf16[128,2,128]{2,1,0:T(2,128)(2,1)S(1)}, u32[]{:S(2)}, u32[]{:S(2)}) async-start(bf16[128,2,128]{2,1,0:T(2,128)(2,1)} %reshape.161), calls=%async_computation.4 | async-start | bytes 131072 | tf_op jit(solution)/shard_map/all_to_all | solution.py:101
  100.9 3.7 %copy-start.2 = (bf16[64,64,512]{2,1,0:T(8,128)(2,1)S(1)}, bf16[64,64,512]{2,1,0:T(8,128)(2,1)}, u32[]{:S(2)}) copy-start(bf16[64,64,512]{2,1,0:T(8,128)(2,1)} %copy-done.1) | copy-start | bytes 12582916
where the time goes:
time: 107 us
  blocking collectives  41.1 us (38%)
  waiting for transfers between devices  20.4 us (19%)
  starting transfers between devices  18 us (17%)
  local copies, waits for them, and re-layouts  11.5 us (11%)
  matrix products  7.93 us (7%)
  other arithmetic  6.95 us (6%)
  between operations  1.11 us (1%)
    all_to_all x1, blocking collectives, sum_at_owner(): lax.all_to_all(parts, axis, split_axis=0, concat_axis=0, tiled=True)  16.3 us
    all_to_all x2, blocking collectives, copy_for_each(): lax.all_to_all(jnp.broadcast_to(x[None], (peers, *x.shape)), axis, 0, 0,...  16.2 us
    all_to_all x1, starting transfers between devices, side_by_side(): lax.all_to_all(both, axis, split_axis=split_dim, concat_axis=concat_dim,...  11.6 us
    all_to_all x1, waiting for transfers between devices, side_by_side(): lax.all_to_all(both, axis, split_axis=split_dim, concat_axis=concat_dim,...  11.1 us
    all_to_all x1, waiting for transfers between devices, backward_cycles(): lax.all_to_all(reduced.astype(jnp.bfloat16), 'blk', split_axis=2, concat_...  9.35 us
    all_gather x1, blocking collectives, in_one_piece(): lax.all_gather(both, axis, axis=dim, tiled=True)  8.64 us
    all_to_all x1, starting transfers between devices, backward_cycles(): lax.all_to_all(reduced.astype(jnp.bfloat16), 'blk', split_axis=2, concat_...  6.4 us
    unnamed x28, local copies, waits for them, and re-layouts  5.97 us
  transfers between devices with their start and end apart: 2, of which 2 were waited for; matrix products, arithmetic and copies ran while one was open for 2% of the time, Pallas kernels for 0%

commit v1 on v0

v1 whole, which is shorter than its diff:
```python
import math

import jax
import jax.numpy as jnp
from jax import lax
from jax.experimental import pallas as pl
from jax.experimental.pallas import tpu as pltpu
from jax.sharding import PartitionSpec as P


def unit_circle(col_ids, mode_ids, cycle_len):
    product_ids = col_ids[:, None] * mode_ids[None, :] % cycle_len
    angles = product_ids.astype(jnp.float32) * (2.0 * math.pi / cycle_len)
    return jnp.cos(angles), jnp.sin(angles)


def phase_tables(first_col, half_len, mode_ids, cycle_len):
    fine_count = 64
    coarse_count = half_len // fine_count
    coarse_cols = first_col + fine_count * jnp.arange(coarse_count, dtype=jnp.int32)
    coarse_cos, coarse_sin = unit_circle(coarse_cols, mode_ids, cycle_len)
    fine_cos, fine_sin = unit_circle(
        jnp.arange(fine_count, dtype=jnp.int32), mode_ids, cycle_len
    )
    coarse_cos, coarse_sin, fine_cos, fine_sin = lax.optimization_barrier(
        (coarse_cos, coarse_sin, fine_cos, fine_sin)
    )
    a, b = coarse_cos[:, None], coarse_sin[:, None]
    c, d = fine_cos[None], fine_sin[None]
    cos_tab = (a * c - b * d).astype(jnp.bfloat16).reshape(half_len, -1)
    sin_tab = (b * c + a * d).astype(jnp.bfloat16).reshape(half_len, -1)
    return lax.optimization_barrier((cos_tab, sin_tab))


def cycle_offsets(cycle_ids, mode_ids, cycle_len):
    parity = (cycle_ids % 2).astype(jnp.float32)
    shifts = math.pi / cycle_len * parity[:, None] * mode_ids[None, :].astype(jnp.float32)
    return (jnp.cos(shifts), jnp.sin(shifts))


NX, NY, NZ = 4, 8, 8
NZL = 4
PLANE = NX * NY
MESH = pl.DeviceIdType.MESH
F32 = jnp.float32
BF16 = jnp.bfloat16


def dot_nn(a, b):
    return jnp.dot(a, b, preferred_element_type=F32)


def dot_nt(a, b):
    return lax.dot_general(a, b, (((1,), (1,)), ((), ())), preferred_element_type=F32)


def iotas(rows, cols):
    row = lax.broadcasted_iota(jnp.int32, (rows, cols), 0)
    col = lax.broadcasted_iota(jnp.int32, (rows, cols), 1)
    return row, col


def one_hot(match):
    return jnp.where(match, 1.0, 0.0).astype(BF16)


def order_rows(h):
    row, col = iotas(256, 128)
    return one_hot(((row >> 3) * 4 + (row & 3) == col) & (((row >> 2) & 1) == h))


def order_cols(h):
    row, col = iotas(128, 256)
    return one_hot(((col >> 3) * 4 + (col & 3) == row) & (((col >> 2) & 1) == h))


def order_first():
    row, col = iotas(256, 256)
    return one_hot(((col & 3) * 64 + ((col >> 2) & 1) * 32 + (col >> 3)) == row)


def order_last():
    row, col = iotas(256, 256)
    return one_hot(((row & 3) * 64 + ((row >> 2) & 1) * 32 + (row >> 3)) == col)


def cycle_order():
    row, col = iotas(256, 256)
    r, x, y, zl, h = row & 1, (row >> 1) & 3, (row >> 3) & 7, (row >> 6) & 1, row >> 7
    return one_hot(r * 128 + zl * 64 + h * 32 + x * 8 + y == col)


def exchange_kernel(
    syn_scale,
    part,
    leg,
    factor,
    wiener_out,
    modes_out,
    leg_p,
    gbuf,
    z_send,
    z_recv,
    y_send,
    y_recv,
    x_recv,
    bx_send,
    bx_recv,
    by_send,
    by_recv,
    bz_send,
    bz_recv,
    send_sem,
    recv_sem,
):
    g, b, zh = lax.axis_index("grp"), lax.axis_index("blk"), lax.axis_index("real")
    x, y, zl = b % NX, (b // NX) % NY, b // PLANE
    z = zh * NZL + zl
    other = 1 - g

    def device(core, zl_, y_, x_, zh_):
        return {"grp": core, "blk": zl_ * PLANE + y_ * NX + x_, "real": zh_}

    z_peers, y_peers, x_peers = [], [], []
    for d in range(1, NZ):
        z_ = (z + d) % NZ
        z_peers.append((z_ % NZL, z_ // NZL, device(g, z_ % NZL, y, x, z_ // NZL)))
    for d in range(1, NY):
        y_ = (y + d) % NY
        y_peers.append((y_, device(g, zl, y_, x, zh)))
    for d in range(NX):
        x_ = (x + d) % NX
        for core in (g, other):
            if d > 0 or core is other:
                x_peers.append((x_, core, device(core, zl, y, x_, zh)))
    core_peer = device(other, zl, y, x, zh)

    barrier = pltpu.get_barrier_semaphore()
    everyone = [p[-1] for p in z_peers] + [p[-1] for p in y_peers] + [p[-1] for p in x_peers]
    for peer in everyone:
        pl.semaphore_signal(barrier, inc=1, device_id=peer, device_id_type=MESH)

    permute = cycle_order()
    for s in range(4):
        leg_p[s] = dot_nn(leg[s], permute).astype(BF16)

    pl.semaphore_wait(barrier, len(everyone))

    sems = iter(range(64))

    def send(src, dst, peer):
        i = next(sems)
        copy = pltpu.make_async_remote_copy(
            src_ref=src,
            dst_ref=dst,
            send_sem=send_sem.at[i],
            recv_sem=recv_sem.at[i],
            device_id=peer,
            device_id_type=MESH,
        )
        copy.start()
        return copy

    sent = []

    def arrive(copies):
        for copy in copies:
            copy.wait_recv()
        sent.extend(copies)

    arrive([send(part.at[other], gbuf, core_peer)])
    for c in range(2):
        total = (part[g, c] + gbuf[c]).astype(BF16)
        for t in range(NZL):
            z_send[t, 16 * c : 16 * (c + 1)] = total[:, 128 * t : 128 * (t + 1)]
    copies = [send(z_send.at[p[0]], z_recv.at[zl, zh], p[2]) for p in z_peers]
    z_recv[zl, zh] = z_send[zl]
    arrive(copies)
    gathered = z_recv[...].reshape(256, 128)
    turned = dot_nt(order_rows(0), gathered[:128]) + dot_nt(order_rows(1), gathered[128:])
    y_send[...] = turned.astype(BF16).reshape(NY, NX, 8, 128)
    copies = [send(y_send.at[p[0]], y_recv.at[y], p[1]) for p in y_peers]
    y_recv[y] = y_send[y]
    arrive(copies)
    copies = [send(y_recv.at[:, p[0]], x_recv.at[g, x], p[2]) for p in x_peers]
    x_recv[g, x] = y_recv[:, x]
    arrive(copies)

    first = order_first()
    columns = [
        dot_nn(first, x_recv[r].reshape(256, 128)).T for r in range(2)
    ]
    scale = factor[...]
    back = []
    for s in range(4):
        rows = jnp.concatenate(
            [
                columns[r][64 * t : 64 * (t + 1), 64 * s : 64 * (s + 1)]
                for r in range(2)
                for t in range(2)
            ],
            axis=1,
        ).astype(BF16)
        wiener = dot_nt(rows, leg_p[s]) * scale
        wiener_out[s] = wiener
        back.append(dot_nn(wiener.astype(BF16), leg_p[s]) * syn_scale)
    last = order_last()
    for r in range(2):
        halves = [
            jnp.concatenate(
                [back[s][:, 128 * r + 64 * t : 128 * r + 64 * (t + 1)] for s in range(4)], axis=1
            )
            for t in range(2)
        ]
        turned = jnp.concatenate(halves, axis=0).T.astype(BF16)
        bx_send[r] = dot_nn(last, turned).astype(BF16).reshape(NX, NY, 8, 128)

    copies = [send(bx_send.at[p[1], p[0]], bx_recv.at[g, x], p[2]) for p in x_peers]
    bx_recv[g, x] = bx_send[g, x]
    arrive(copies)
    by_send[...] = (bx_recv[0].astype(F32) + bx_recv[1].astype(F32)).astype(BF16)
    copies = [send(by_send.at[:, p[0]], by_recv.at[y], p[1]) for p in y_peers]
    by_recv[y] = by_send[:, y]
    arrive(copies)
    plane = by_recv[...].reshape(256, 128)
    for h in range(2):
        turned = dot_nn(order_cols(h), plane).T.astype(BF16)
        bz_send[2 * h : 2 * h + 2] = turned.reshape(2, 2, 32, 128)
    copies = [send(bz_send.at[p[0], p[1]], bz_recv.at[zl, zh], p[2]) for p in z_peers]
    bz_recv[zl, zh] = bz_send[zl, zh]
    arrive(copies)
    for t in range(NZL):
        modes_out[g, :, 128 * t : 128 * (t + 1)] = (
            bz_recv[t, 0].astype(F32) + bz_recv[t, 1].astype(F32)
        ).astype(BF16)
    arrive([send(modes_out.at[g], modes_out.at[g], core_peer)])
    for copy in sent:
        copy.wait_send()


def exchange(part, legendre, factor, syn_scale):
    def vmem(shape, dtype=BF16):
        return pltpu.VMEM(shape, dtype)

    block = pl.BlockSpec(memory_space=pltpu.VMEM)
    plane = (NX, NY, 8, 128)
    return pl.pallas_call(
        lambda *refs: exchange_kernel(syn_scale, *refs),
        out_shape=(
            jax.ShapeDtypeStruct((4, 64, 1024), F32),
            jax.ShapeDtypeStruct((2, 32, 512), BF16),
        ),
        in_specs=[block] * 3,
        out_specs=(block, block),
        scratch_shapes=[
            vmem((4, 1024, 256)),
            vmem((2, 16, 512), F32),
            vmem((NZL, 32, 128)),
            vmem((NZL, 2, 32, 128)),
            vmem((NY, NX, 8, 128)),
            vmem((NY, NX, 8, 128)),
            vmem((2, NX, NY, 8, 128)),
            vmem((2, NX, NY, 8, 128)),
            vmem((2, NX, NY, 8, 128)),
            vmem((NX, NY, 8, 128)),
            vmem((NY, NX, 8, 128)),
            vmem((NZL, 2, 32, 128)),
            vmem((NZL, 2, 32, 128)),
            pltpu.SemaphoreType.DMA((64,)),
            pltpu.SemaphoreType.DMA((64,)),
        ],
        compiler_params=pltpu.CompilerParams(
            collective_id=0, has_side_effects=True, vmem_limit_bytes=40 * 1024 * 1024
        ),
    )(part, legendre, factor)


def per_device(
    sky_data, signal_prev, noise_var, mask_flags, cycle_table, m_table, spectrum, legendre
):
    real_dev, cycle_dev, half_len = sky_data.shape
    cycle_len = half_len * lax.axis_size("grp")
    mode_count = m_table.shape[0]
    first_col = lax.axis_index("grp") * half_len
    cos_tab, sin_tab = phase_tables(first_col, half_len, m_table, cycle_len)
    cos_shift, sin_shift = cycle_offsets(cycle_table, m_table, cycle_len)
    cos_rows, sin_rows = cos_shift[:, None], sin_shift[:, None]
    weight = mask_flags.astype(F32) / (noise_var - 0.5)
    messenger = (weight * sky_data + 2.0 * signal_prev) / (weight + 2.0)
    flat_rows = messenger.astype(BF16).transpose(1, 0, 2).reshape(-1, half_len)
    base_cos = dot_nn(flat_rows, cos_tab).reshape(cycle_dev, real_dev, mode_count)
    base_sin = -dot_nn(flat_rows, sin_tab).reshape(cycle_dev, real_dev, mode_count)
    norm_scale = cycle_len ** (-0.5)
    re_part = (base_cos * cos_rows + base_sin * sin_rows) * norm_scale
    im_part = (base_sin * cos_rows - base_cos * sin_rows) * norm_scale
    part = jnp.stack([re_part, im_part], 1)
    factor = (spectrum / (spectrum + 0.5))[None]
    total_l = legendre.shape[1] * lax.axis_size("grp") * lax.axis_size("real")
    syn_scale = (legendre.shape[2] / total_l) ** 0.5
    wiener, modes = exchange(part, legendre, factor, syn_scale)
    wiener_alm = (
        wiener.reshape(4, 2, 2, 16, 1024).transpose(1, 3, 2, 0, 4).reshape(32, 2, 4, 1024)
    )
    modes = modes.astype(F32).reshape(cycle_dev, 2, real_dev, mode_count)
    modes_re, modes_im = modes[:, 0], modes[:, 1]
    rotated_re = (modes_re * cos_rows - modes_im * sin_rows).astype(BF16)
    rotated_im = (modes_im * cos_rows + modes_re * sin_rows).astype(BF16)
    pixel_sum = dot_nt(rotated_re.reshape(-1, mode_count), cos_tab)
    pixel_sum = pixel_sum - dot_nt(rotated_im.reshape(-1, mode_count), sin_tab)
    signal_next = (pixel_sum * mode_count ** (-0.5)).reshape(cycle_dev, real_dev, half_len)
    return (wiener_alm, signal_next.transpose(1, 0, 2))


def solution(mesh):
    in_specs = (
        P("real", "blk", "grp"),
        P("real", "blk", "grp"),
        P("blk", "grp"),
        P("blk", "grp"),
        P("blk"),
        P(),
        P(("grp", "real")),
        P("blk", ("grp", "real"), None),
    )
    out_specs = (P(None, None, "blk", ("grp", "real")), P("real", "blk", "grp"))
    return jax.shard_map(
        per_device, mesh=mesh, in_specs=in_specs, out_specs=out_specs, check_vma=False
    )
```

time: 107 us -> 62.2 us (0.58)
  Pallas kernels: 0 us -> 47.8 us
  blocking collectives: 41.1 us -> 0 us
  waiting for transfers between devices: 20.4 us -> 0 us
  starting transfers between devices: 18 us -> 0 us
  local copies, waits for them, and re-layouts: 11.5 us -> 3.4 us
  matrix products: 7.93 us -> 4.37 us
  other arithmetic: 6.95 us -> 5.55 us
    pallas_call x0 -> x1, Pallas kernels: none -> 47.8 us  [exchange(): pl.pallas_call(lambda *refs: exchange_kernel(syn_scale, *refs), out_shape...]
    all_to_all x3 -> x0, blocking collectives: 32.5 us -> none  [the longest x1 16.3 us: sum_at_owner(): lax.all_to_all(parts, axis, split_axis=0, concat_axis=0, tiled=True)]
    all_to_all x2 -> x0, waiting for transfers between devices: 20.4 us -> none  [the longest x1 11.1 us: side_by_side(): lax.all_to_all(both, axis, split_axis=split_dim, concat_axis=concat_dim,...]
    all_to_all x2 -> x0, starting transfers between devices: 18 us -> none  [the longest x1 11.6 us: side_by_side(): lax.all_to_all(both, axis, split_axis=split_dim, concat_axis=concat_dim,...]
    all_gather x1 -> x0, blocking collectives: 8.64 us -> none  [in_one_piece(): lax.all_gather(both, axis, axis=dim, tiled=True)]
    unnamed x28 -> x16, local copies, waits for them, and re-layouts: 5.97 us -> 0.54 us
    dot_general x6 -> x4, matrix products: 7.93 us -> 4.37 us  [the longest x2 2.65 us: dot_nt(): lax.dot_general(a, b, (((1,), (1,)), ((), ())), preferred_element_type=F32)]
    convert_element_type x5 -> x0, local copies, waits for them, and re-layouts: 2 us -> none  [the longest x1 1.07 us: backward_cycles(): reduced.astype(jnp.bfloat16)]
  transfers between devices with their start and end apart: 2 -> 0, of which waited for: 2 -> 0; matrix products, arithmetic and copies ran while one was open for 2% -> 0% of each run, Pallas kernels for 0% -> 0%
where the time goes in v1:
time: 62.2 us; the launch traced here: 62 us
  Pallas kernels  47.8 us (77%)
  other arithmetic  5.55 us (9%)
  matrix products  4.37 us (7%)
  local copies, waits for them, and re-layouts  3.4 us (5%)
  between operations  0.85 us (1%)
    pallas_call x1, Pallas kernels, exchange(): pl.pallas_call(lambda *refs: exchange_kernel(syn_scale, *refs), out_shape...  47.8 us
    convert_element_type x1, other arithmetic, phase_tables(): sin_tab = (b * c + a * d).astype(jnp.bfloat16).reshape(half_len, -1)  3.17 us
    dot_general x2, matrix products, dot_nt(): lax.dot_general(a, b, (((1,), (1,)), ((), ())), preferred_element_type=F32)  2.65 us
    sin x1, other arithmetic, unit_circle(): return (jnp.cos(angles), jnp.sin(angles))  1.74 us
    dot_general x2, matrix products, dot_nn(): return jnp.dot(a, b, preferred_element_type=F32)  1.73 us
    transpose x1, local copies, waits for them, and re-layouts, per_device(): wiener.reshape(4, 2, 2, 16, 1024).transpose(1, 3, 2, 0, 4)  1.65 us

profile of v1, /device:TPU:1, one launch (start us, length us, event | category | flops | bytes accessed | tf_op | source)
XLA Modules:
  0.0 62.0 jit_solution(17528909530961756583)
XLA Ops:
  0.6 1.7 %fusion.27 = (f32[64,512]{1,0:T(8,128)S(1)}, f32[64,512]{1,0:T(8,128)S(1)}, f32[64,512]{1,0:T(8,128)S(1)}, f32[64,512]{1,0:T(8,128)S(1)}) fusion(s32[512]{0:T(512)} %param.13, s32[64]{0:T(128)S(1)} %multiply_add_fusion), kind=kLoop, calls=%fused_computation.45 | loop fusion | flops 917504 | bytes 526592 | tf_op jit(solution)/shard_map/sin | solution.py:14
  2.4 0.0 copy-start.3
  2.4 0.0 copy-start.4
  2.4 0.0 copy-start.1
  2.4 0.0 copy-start.2
  2.4 3.2 %add_convert_fusion = (bf16[64,64,512]{2,1,0:T(8,128)(2,1)S(1)}, bf16[64,64,512]{2,1,0:T(8,128)(2,1)S(1)}) fusion(f32[64,512]{1,0:T(8,128)S(1)} %get-tuple-element.13, f32[64,512]{1,0:T(8,128)S(1)} %get-tuple-element.12, f32[64,512]{1,0:T(8,128)S(1)} %get-tuple-element.11, f32[64,512]{1,0:T(8,128)S(1)} %get-tuple-element.10), kind=kLoop, calls=%fused_computation | loop fusion | flops 16777216 | bytes 8912896 | tf_op jit(solution)/shard_map/convert_element_type | solution.py:31
  5.6 0.0 copy-start.5
  5.6 0.0 copy-start.7
  5.6 0.0 copy-done.3
  5.6 0.0 copy-done.4
  5.7 0.0 copy-done.1
  5.7 0.4 fusion.9
  6.1 0.9 %fusion.3 = f32[2,16,512]{2,1,0:T(8,128)S(1)} fusion(bf16[4096,512]{1,0:T(8,128)(2,1)S(1)} %bitcast.64, bf16[2,16,4096]{2,0,1:T(2,128)(2,1)S(1)} %fusion.9), kind=kOutput, calls=%fused_computation.6 | convolution fusion | flops 134217728 | bytes 4521984 | tf_op jit(solution)/shard_map/dot_general | solution.py:50
  7.0 0.0 copy-done.5
  7.0 0.0 copy-start.6
  7.0 0.0 copy-start
  7.0 0.1 multiply_cosine_fusion
  7.2 0.9 %multiply_bitcast_fusion.1 = (f32[2,1,16,512]{3,2,1,0:T(8,128)S(1)}, f32[2,1,16,512]{3,2,1,0:T(8,128)S(1)}) fusion(f32[2,16,512]{2,1,0:T(8,128)S(1)} %fusion.3, f32[2,512]{1,0:T(2,128)S(1)} %get-tuple-element.29, f32[2,512]{1,0:T(2,128)S(1)} %get-tuple-element.28, bf16[4096,512]{1,0:T(8,128)(2,1)S(1)} %bitcast.62, bf16[2,16,4096]{2,0,1:T(2,128)(2,1)S(1)} %fusion.9), kind=kOutput, calls=%fused_computation.42 | convolution fusion | flops 134365184 | bytes 4661248 | tf_op jit(solution)/shard_map/dot_general | solution.py:50
  8.1 0.5 copy-done
  8.6 47.8 %shard_map.95 = (f32[4,64,1024]{2,1,0:T(8,128)S(1)}, bf16[2,32,512]{2,1,0:T(8,128)(2,1)S(1)}) custom-call(f32[2,2,16,512]{3,2,1,0:T(8,128)S(1)} %pad_maximum_fusion.refs_0_, bf16[4,1024,256]{2,1,0:T(8,128)(2,1)S(1)} %copy-done, f32[1,1024]{1,0:T(1,128)S(1)} %bitcast.61), custom_call_target="tpu_custom_call" | custom-call | tf_op jit(solution)/shard_map/pallas_call | solution.py:247
  56.5 1.3 %fusion.37 = f32[32,4096]{1,0:T(8,128)S(1)} fusion(bf16[32,512]{1,0:T(8,128)(2,1)S(1)} %get-tuple-element.23, bf16[4096,512]{1,0:T(8,128)(2,1)S(1)} %bitcast.65), kind=kOutput, calls=%fused_computation.60 | convolution fusion | flops 134217728 | bytes 4751360 | tf_op jit(solution)/shard_map/dot_general | solution.py:54
  57.8 1.3 %fusion = f32[32,4096]{1,0:T(8,128)S(1)} fusion(f32[32,4096]{1,0:T(8,128)S(1)} %fusion.37, bf16[32,512]{1,0:T(8,128)(2,1)S(1)} %get-tuple-element.22, bf16[4096,512]{1,0:T(8,128)(2,1)S(1)} %bitcast.63), kind=kOutput, calls=%fused_computation.3 | convolution fusion | flops 134479872 | bytes 5275648 | tf_op jit(solution)/shard_map/dot_general | solution.py:54
  59.1 1.2 %copy.22 = f32[2,16,4096]{2,0,1:T(2,128)} copy(f32[2,16,4096]{2,1,0:T(8,128)S(1)} %bitcast.66) | data formatting | bytes 1048576 | tf_op jit(solution)/shard_map/reshape | solution.py:310
  60.3 1.6 %copy.13 = f32[2,16,2,4,1024]{4,3,2,1,0:T(4,128)} copy(f32[2,16,2,4,1024]{4,1,2,0,3:T(8,128)S(1)} %bitcast.59) | data formatting | bytes 2097152 | tf_op jit(solution)/shard_map/transpose | solution.py:302
  (11 shorter events, 0.1 us)
Async XLA Ops:
  2.4 3.3 %copy-start.3 = (f32[2,4096]{1,0:T(2,128)S(1)}, f32[2,4096]{1,0:T(2,128)}, u32[]{:S(2)}) copy-start(f32[2,4096]{1,0:T(2,128)} %param.10) | copy-start | bytes 98308
  2.4 3.3 %copy-start.4 = (s32[2,4096]{1,0:T(2,128)S(1)}, s32[2,4096]{1,0:T(2,128)}, u32[]{:S(2)}) copy-start(s32[2,4096]{1,0:T(2,128)} %param.11) | copy-start | bytes 98308
  2.4 3.3 %copy-start.1 = (f32[16,2,4096]{2,1,0:T(2,128)S(1)}, f32[16,2,4096]{2,1,0:T(2,128)}, u32[]{:S(2)}) copy-start(f32[16,2,4096]{2,1,0:T(2,128)} %param.9) | copy-start | bytes 1572868
  2.4 3.3 %copy-start.2 = (f32[16,2,4096]{2,1,0:T(2,128)S(1)}, f32[16,2,4096]{2,1,0:T(2,128)}, u32[]{:S(2)}) copy-start(f32[16,2,4096]{2,1,0:T(2,128)} %param.8) | copy-start | bytes 1572868
  5.6 1.4 %copy-start.5 = (s32[512]{0:T(512)S(1)}, s32[512]{0:T(512)}, u32[]{:S(2)}) copy-start(s32[512]{0:T(512)} %param.13) | copy-start | bytes 6148
  5.6 1.4 %copy-start.7 = (s32[2]{0:T(128)S(1)}, s32[2]{0:T(128)}, u32[]{:S(2)}) copy-start(s32[2]{0:T(128)} %param.12) | copy-start | bytes 28
  7.0 1.1 %copy-start.6 = (f32[1024]{0:T(1024)S(1)}, f32[1024]{0:T(1024)}, u32[]{:S(2)}) copy-start(f32[1024]{0:T(1024)} %param.14) | copy-start | bytes 12292
  7.0 1.6 %copy-start = (bf16[4,1024,256]{2,1,0:T(8,128)(2,1)S(1)}, bf16[4,1024,256]{2,1,0:T(8,128)(2,1)}, u32[]{:S(2)}) copy-start(bf16[4,1024,256]{2,1,0:T(8,128)(2,1)} %refs_1_.1) | copy-start | bytes 6291460

commit v2 on v1

v2 whole, which is shorter than its diff:
```python
import math

import jax
import jax.numpy as jnp
from jax import lax
from jax.experimental import pallas as pl
from jax.experimental.pallas import tpu as pltpu
from jax.sharding import PartitionSpec as P


NX, NY, NZ = 4, 8, 8
NZL = 4
PLANE = NX * NY
BLOCKS = 8
SPAN = 512
ORDERS = 512
TURN = 16384
MESH = pl.DeviceIdType.MESH
F32 = jnp.float32
BF16 = jnp.bfloat16


def dot_nn(a, b):
    return jnp.dot(a, b, preferred_element_type=F32)


def dot_nt(a, b):
    return lax.dot_general(a, b, (((1,), (1,)), ((), ())), preferred_element_type=F32)


def iotas(rows, cols):
    row = lax.broadcasted_iota(jnp.int32, (rows, cols), 0)
    col = lax.broadcasted_iota(jnp.int32, (rows, cols), 1)
    return row, col


def one_hot(match):
    return jnp.where(match, 1.0, 0.0).astype(BF16)


def order_rows(h):
    row, col = iotas(256, 128)
    return one_hot(((row >> 3) * 4 + (row & 3) == col) & (((row >> 2) & 1) == h))


def order_cols(h):
    row, col = iotas(128, 256)
    return one_hot(((col >> 3) * 4 + (col & 3) == row) & (((col >> 2) & 1) == h))


def order_first():
    row, col = iotas(256, 256)
    return one_hot(((col & 3) * 64 + ((col >> 2) & 1) * 32 + (col >> 3)) == row)


def order_last():
    row, col = iotas(256, 256)
    x, y = (row >> 3) & 3, row >> 5
    return one_hot(((row & 3) * 64 + ((row >> 2) & 1) * 32 + x * 8 + y) == col)


def cycle_order():
    row, col = iotas(256, 256)
    r, x, y, zl, h = row & 1, (row >> 1) & 3, (row >> 3) & 7, (row >> 6) & 1, row >> 7
    return one_hot(r * 128 + zl * 64 + h * 32 + x * 8 + y == col)


def circle(steps):
    u = (steps + TURN // 8) & (TURN - 1)
    quad = u // (TURN // 4)
    t = ((u & (TURN // 4 - 1)) - TURN // 8).astype(F32) * (2.0 * math.pi / TURN)
    q = t * t
    sine = t * (1.0 + q * (-1 / 6 + q * (1 / 120 + q * (-1 / 5040 + q * (1 / 362880)))))
    cosine = 1.0 + q * (-1 / 2 + q * (1 / 24 + q * (-1 / 720 + q * (1 / 40320))))
    odd = (quad & 1) == 1
    cos = jnp.where(odd, sine, cosine)
    sin = jnp.where(odd, cosine, sine)
    cos = jnp.where((quad == 1) | (quad == 2), -cos, cos)
    return cos, jnp.where(quad >= 2, -sin, sin)


def ring_distance(d, n):
    return min(d, n - d)


Z_STEPS = sorted(range(1, NZ), key=lambda d: -ring_distance(d, NZ))
PLANE_STEPS = sorted(
    [(e, d) for e in range(NY) for d in range(NX) if e or d],
    key=lambda p: -(ring_distance(p[0], NY) + ring_distance(p[1], NX)),
)


def step_kernel(
    syn_scale,
    sky_hbm,
    prev_hbm,
    noise_hbm,
    mask_hbm,
    cycles_hbm,
    m_hbm,
    spectrum_hbm,
    leg_hbm,
    wiener_out,
    signal_out,
    sky,
    prev,
    noise,
    mask,
    cycles,
    m_ref,
    spectrum,
    blocks,
    table,
    phase_cos,
    phase_sin,
    part,
    leg,
    leg_p,
    core_buf,
    z_send,
    z_recv,
    p_send,
    p_recv,
    back,
    back_buf,
    q_send,
    q_recv,
    w_send,
    w_recv,
    modes,
    rotated,
    send_sem,
    recv_sem,
    load_sem,
):
    g, b, zh = lax.axis_index("grp"), lax.axis_index("blk"), lax.axis_index("real")
    x, y, zl = b % NX, (b // NX) % NY, b // PLANE
    z = zh * NZL + zl
    other = 1 - g
    ys = [(y + e) % NY for e in range(NY)]
    xs = [(x + d) % NX for d in range(NX)]

    core_peer = {"grp": other}
    z_peers = []
    for d in Z_STEPS:
        z_ = (z + d) % NZ
        z_peers.append((z_ % NZL, z_ // NZL, {"blk": (z_ % NZL) * PLANE + b % PLANE, "real": z_ // NZL}))
    plane_peers = [
        (ys[e] * NX + xs[d], {"blk": zl * PLANE + ys[e] * NX + xs[d]}) for e, d in PLANE_STEPS
    ]
    here = b % PLANE

    loads = [
        pltpu.make_async_copy(src, dst, load_sem.at[i])
        for i, (src, dst) in enumerate(
            [
                (m_hbm, m_ref),
                (cycles_hbm, cycles),
                (noise_hbm, noise),
                (mask_hbm, mask),
                (sky_hbm, sky),
                (prev_hbm, prev),
                (spectrum_hbm, spectrum),
                (leg_hbm, leg),
            ]
        )
    ]
    for load in loads:
        load.start()
    barrier = pltpu.get_barrier_semaphore()
    everyone = [core_peer] + [p[-1] for p in z_peers] + [p[-1] for p in plane_peers]
    for peer in everyone:
        pl.semaphore_signal(barrier, inc=1, device_id=peer, device_id_type=MESH)

    loads[0].wait()
    m = m_ref[...]
    fine_row = lax.broadcasted_iota(jnp.int32, (32, ORDERS), 0)
    row = lax.broadcasted_iota(jnp.int32, (16, ORDERS), 0)
    fine_cos, fine_sin = circle(m * fine_row * 2)
    coarse_cos, coarse_sin = circle(m * row * 64)
    for a in range(SPAN // 32):
        ca, sa = coarse_cos[a : a + 1], coarse_sin[a : a + 1]
        rows = slice(32 * a, 32 * (a + 1))
        table[rows, :ORDERS] = (ca * fine_cos - sa * fine_sin).astype(BF16)
        table[rows, ORDERS:] = (sa * fine_cos + ca * fine_sin).astype(BF16)
    loads[1].wait()
    parity = jnp.where((row & 1) == 1, cycles[:, 1:2], cycles[:, 0:1]) & 1
    pixel = g * (BLOCKS * SPAN) + (row >> 1) * SPAN
    pc, ps = circle(m * ((2 * pixel + parity) & (TURN - 1)))
    phase_cos[...] = pc
    phase_sin[...] = ps

    for load in loads[2:6]:
        load.wait()
    weight = mask[...].astype(F32) / (noise[...] - 0.5)
    of_prev = 2.0 / (weight + 2.0)
    of_sky = weight / (weight + 2.0)
    for i in range(64):
        tile, r = i // 2, i % 2
        at = pl.Slice(i, 16, 64)
        value = of_sky[i : i + 1] * sky[at, :] + of_prev[i : i + 1] * prev[at, :]
        q, t = tile // 4, tile % 4
        blocks[16 * (2 * q + r) : 16 * (2 * q + r + 1), 128 * t : 128 * (t + 1)] = value.astype(
            BF16
        )
    norm = (2 * BLOCKS * SPAN) ** -0.5
    for n in range(2):
        cols = slice(256 * n, 256 * (n + 1))
        sum_cos = dot_nn(blocks[...], table[:, 256 * n : 256 * (n + 1)])
        sum_sin = dot_nn(blocks[...], table[:, ORDERS + 256 * n : ORDERS + 256 * (n + 1)])
        for r in range(2):
            re = jnp.zeros((16, 256), F32)
            im = jnp.zeros((16, 256), F32)
            for q in range(BLOCKS):
                i = 2 * q + r
                c, s = pc[i : i + 1, cols], ps[i : i + 1, cols]
                yc, ys_ = sum_cos[16 * i : 16 * (i + 1)], sum_sin[16 * i : 16 * (i + 1)]
                re = re + (yc * c - ys_ * s)
                im = im - (ys_ * c + yc * s)
            part[r, 0, :, cols] = re * norm
            part[r, 1, :, cols] = im * norm

    pl.semaphore_wait(barrier, len(everyone))

    def send(phase, src, dst, peer):
        pltpu.make_async_remote_copy(
            src_ref=src,
            dst_ref=dst,
            send_sem=send_sem.at[phase],
            recv_sem=recv_sem.at[phase],
            device_id=peer,
            device_id_type=MESH,
        ).start()

    def keep(phase, src, dst):
        pltpu.make_async_copy(src, dst, recv_sem.at[phase]).start()

    def arrived(phase, ref):
        pltpu.make_async_copy(ref, ref, recv_sem.at[phase]).wait()

    def left(phase, ref):
        pltpu.make_async_copy(ref, ref, send_sem.at[phase]).wait()

    send(0, part.at[other], core_buf, core_peer)
    arrived(0, core_buf)
    for c in range(2):
        total = (part[g, c] + core_buf[c]).astype(BF16)
        for t in range(NZL):
            z_send[t, 16 * c : 16 * (c + 1)] = total[:, 128 * t : 128 * (t + 1)]
    for zl_, zh_, peer in z_peers:
        send(1, z_send.at[zl_], z_recv.at[2 * zl + zh], peer)
    keep(1, z_send.at[zl], z_recv.at[2 * zl + zh])
    loads[7].wait()
    permute = cycle_order()
    for s in range(4):
        leg_p[s] = dot_nn(leg[s], permute).astype(BF16)
    arrived(1, z_recv)
    gathered = z_recv[...].reshape(256, 128)
    turned = dot_nt(order_rows(0), gathered[:128]) + dot_nt(order_rows(1), gathered[128:])
    p_send[...] = turned.astype(BF16).reshape(PLANE, 8, 128)
    slot = x * NY + y
    for i, peer in plane_peers:
        send(2, p_send.at[i], p_recv.at[g, slot], peer)
    keep(2, p_send.at[here], p_recv.at[g, slot])
    arrived(2, p_recv.at[g])
    send(3, p_recv.at[g], p_recv.at[g], core_peer)
    arrived(3, p_recv.at[other])

    first = order_first()
    columns = [
        dot_nn(first, p_recv[r].reshape(256, 128)).T for r in range(2)
    ]
    loads[6].wait()
    power = spectrum[...]
    scale = power / (power + 0.5)
    for s in range(4):
        rows = jnp.concatenate(
            [
                columns[r][64 * t : 64 * (t + 1), 64 * s : 64 * (s + 1)]
                for r in range(2)
                for t in range(2)
            ],
            axis=1,
        ).astype(BF16)
        wiener = dot_nt(rows, leg_p[s]) * scale
        for p in range(4):
            for t in range(8):
                wiener_out[pl.Slice((p // 2) * 1024 + (p % 2) * 32 + t * 4 + s, 16, 64), :] = wiener[
                    16 * p : 16 * (p + 1), 128 * t : 128 * (t + 1)
                ]
        partial = dot_nn(wiener.astype(BF16), leg_p[s]) * syn_scale
        back[0, s] = partial[:, :128]
        back[1, s] = partial[:, 128:]

    send(4, back.at[other], back_buf, core_peer)
    arrived(4, back_buf)
    both = back[g] + back_buf[...]
    halves = [
        jnp.concatenate([both[s][:, 64 * t : 64 * (t + 1)] for s in range(4)], axis=1)
        for t in range(2)
    ]
    turned = jnp.concatenate(halves, axis=0).T.astype(BF16)
    q_send[...] = dot_nn(order_last(), turned).astype(BF16).reshape(PLANE, 8, 128)
    for i, peer in plane_peers:
        send(5, q_send.at[i], q_recv.at[here], peer)
    keep(5, q_send.at[here], q_recv.at[here])
    arrived(5, q_recv)
    plane = q_recv[...].reshape(256, 128)
    for h in range(2):
        turned = dot_nn(order_cols(h), plane).T.astype(BF16)
        w_send[4 * h : 4 * h + 4] = turned.reshape(4, 32, 128)
    for zl_, zh_, peer in z_peers:
        send(6, w_send.at[2 * zl_ + zh_], w_recv.at[2 * zl + zh], peer)
    keep(6, w_send.at[2 * zl + zh], w_recv.at[2 * zl + zh])
    arrived(6, w_recv)
    for t in range(NZL):
        modes[g, :, 128 * t : 128 * (t + 1)] = (
            w_recv[2 * t].astype(F32) + w_recv[2 * t + 1].astype(F32)
        ).astype(BF16)
    send(7, modes.at[g], modes.at[g], core_peer)
    arrived(7, modes.at[other])

    for r in range(2):
        re, im = modes[r, :16].astype(F32), modes[r, 16:].astype(F32)
        for q in range(BLOCKS):
            i = 2 * q + r
            c, s = phase_cos[i : i + 1], phase_sin[i : i + 1]
            rotated[16 * i : 16 * (i + 1), :ORDERS] = (re * c - im * s).astype(BF16)
            rotated[16 * i : 16 * (i + 1), ORDERS:] = (-(im * c + re * s)).astype(BF16)
    for n in range(2):
        pixels = dot_nt(rotated[...], table[256 * n : 256 * (n + 1)]) * ORDERS**-0.5
        for i in range(2 * BLOCKS):
            for t in range(2):
                start = ((i // 2) * 4 + 2 * n + t) * 2 + i % 2
                signal_out[pl.Slice(start, 16, 64), :] = pixels[
                    16 * i : 16 * (i + 1), 128 * t : 128 * (t + 1)
                ]

    left(0, core_buf)
    left(1, z_recv.at[0:7])
    left(2, p_recv.at[0, 0:31])
    left(3, p_recv.at[0])
    left(4, back_buf)
    left(5, q_recv.at[0:31])
    left(6, w_recv.at[0:7])
    left(7, modes.at[0])


def step(inputs, syn_scale):
    def vmem(shape, dtype=BF16):
        return pltpu.VMEM(shape, dtype)

    block = pl.BlockSpec(memory_space=pltpu.VMEM)
    return pl.pallas_call(
        lambda *refs: step_kernel(syn_scale, *refs),
        out_shape=(
            jax.ShapeDtypeStruct((2048, 128), F32),
            jax.ShapeDtypeStruct((1024, 128), F32),
        ),
        in_specs=[pl.BlockSpec(memory_space=pltpu.HBM)] * 8,
        out_specs=(block, block),
        scratch_shapes=[
            vmem((1024, 128), F32),
            vmem((1024, 128), F32),
            vmem((64, 128), F32),
            vmem((64, 128), jnp.int32),
            vmem((1, 2), jnp.int32),
            vmem((1, ORDERS), jnp.int32),
            vmem((1, 1024), F32),
            vmem((32 * BLOCKS, SPAN)),
            vmem((SPAN, 2 * ORDERS)),
            vmem((16, ORDERS), F32),
            vmem((16, ORDERS), F32),
            vmem((2, 2, 16, ORDERS), F32),
            vmem((4, 1024, 256)),
            vmem((4, 1024, 256)),
            vmem((2, 16, ORDERS), F32),
            vmem((NZL, 32, 128)),
            vmem((NZ, 32, 128)),
            vmem((PLANE, 8, 128)),
            vmem((2, PLANE, 8, 128)),
            vmem((2, 4, 64, 128), F32),
            vmem((4, 64, 128), F32),
            vmem((PLANE, 8, 128)),
            vmem((PLANE, 8, 128)),
            vmem((NZ, 32, 128)),
            vmem((NZ, 32, 128)),
            vmem((2, 32, ORDERS)),
            vmem((32 * BLOCKS, 2 * ORDERS)),
            pltpu.SemaphoreType.DMA((8,)),
            pltpu.SemaphoreType.DMA((8,)),
            pltpu.SemaphoreType.DMA((8,)),
        ],
        compiler_params=pltpu.CompilerParams(
            collective_id=0, has_side_effects=True, vmem_limit_bytes=67043328
        ),
    )(*inputs)


def per_device(
    sky_data, signal_prev, noise_var, mask_flags, cycle_table, m_table, spectrum, legendre
):
    half_len = sky_data.shape[2]
    total_l = legendre.shape[1] * lax.axis_size("grp") * lax.axis_size("real")
    syn_scale = (legendre.shape[2] / total_l) ** 0.5

    def rows(a):
        return a.reshape(-1, 2, half_len // 128, 128).swapaxes(1, 2).reshape(-1, 128)

    inputs = (
        rows(sky_data),
        rows(signal_prev),
        rows(noise_var),
        rows(mask_flags),
        cycle_table[None],
        m_table[None],
        spectrum[None],
        legendre,
    )
    wiener, signal = step(inputs, syn_scale)
    wiener_alm = (
        wiener.reshape(32, 2, 8, 4, 128).transpose(0, 1, 3, 2, 4).reshape(32, 2, 4, 1024)
    )
    signal_next = signal.reshape(16, 32, 2, 128).transpose(0, 2, 1, 3).reshape(16, 2, half_len)
    return (wiener_alm, signal_next)


def solution(mesh):
    in_specs = (
        P("real", "blk", "grp"),
        P("real", "blk", "grp"),
        P("blk", "grp"),
        P("blk", "grp"),
        P("blk"),
        P(),
        P(("grp", "real")),
        P("blk", ("grp", "real"), None),
    )
    out_specs = (P(None, None, "blk", ("grp", "real")), P("real", "blk", "grp"))
    return jax.shard_map(
        per_device, mesh=mesh, in_specs=in_specs, out_specs=out_specs, check_vma=False
    )
```

time: 62.2 us -> 49.8 us (0.80)
  other arithmetic: 5.55 us -> 0 us
  matrix products: 4.37 us -> 0 us
  Pallas kernels: 47.8 us -> 45.9 us
    dot_general x4 -> x0, matrix products: 4.37 us -> none  [the longest x2 2.65 us: dot_nt(): lax.dot_general(a, b, (((1,), (1,)), ((), ())), preferred_element_type=F32)]
    convert_element_type x3 -> x0, other arithmetic: 3.2 us -> none  [the longest x1 3.17 us: phase_tables(): sin_tab = (b * c + a * d).astype(jnp.bfloat16).reshape(half_len, -1)]
    unnamed x16 -> x4, local copies, waits for them, and re-layouts: 0.54 us -> 3.16 us
    pallas_call x1, Pallas kernels: 47.8 us -> 45.9 us  [step(): pl.pallas_call(lambda *refs: step_kernel(syn_scale, *refs), out_shape=(ja...]
    sin x1 -> x0, other arithmetic: 1.74 us -> none  [unit_circle(): return (jnp.cos(angles), jnp.sin(angles))]
    transpose x1 -> x0, local copies, waits for them, and re-layouts: 1.65 us -> none  [per_device(): wiener.reshape(4, 2, 2, 16, 1024).transpose(1, 3, 2, 0, 4)]
    reshape x1 -> x0, local copies, waits for them, and re-layouts: 1.2 us -> none  [per_device(): (pixel_sum * mode_count ** (-0.5)).reshape(cycle_dev, real_dev, half_len)]
where the time goes in v2:
time: 49.8 us; the launch traced here: 49.7 us
  Pallas kernels  45.9 us (92%)
  local copies, waits for them, and re-layouts  3.16 us (6%)
  between operations  0.65 us (1%)
    pallas_call x1, Pallas kernels, step(): pl.pallas_call(lambda *refs: step_kernel(syn_scale, *refs), out_shape=(ja...  45.9 us
    unnamed x4, local copies, waits for them, and re-layouts  3.16 us

profile of v2, /device:TPU:1, one launch (start us, length us, event | category | flops | bytes accessed | tf_op | source)
XLA Modules:
  0.0 49.7 jit_solution(4877845784315451665)
XLA Ops:
  0.6 45.9 %shard_map.95 = (f32[2048,128]{1,0:T(8,128)}, f32[1024,128]{1,0:T(8,128)}) custom-call(f32[1024,128]{1,0:T(8,128)} %bitcast.35, f32[1024,128]{1,0:T(8,128)} %bitcast.36, f32[64,128]{1,0:T(8,128)} %bitcast.37, s32[64,128]{1,0:T(8,128)} %bitcast.38, s32[1,2]{1,0:T(1,128)} %bitcast.41, s32[1,512]{1,0:T(1,128)} %bitcast.40, f32[1,1024]{1,0:T(1,128)} %bitcast.39, ...), custom_call_target="tpu_custom_call" | custom-call | tf_op jit(solution)/shard_map/pallas_call | solution.py:354
  46.5 0.0 copy-start
  46.5 2.4 %copy.18 = f32[32,2,4,1024]{3,2,1,0:T(4,128)} copy(f32[32,2,4,1024]{3,2,1,0:T(4,128)} %bitcast.33) | data formatting | bytes 2097152
  48.9 0.0 copy-done
  48.9 0.8 %copy.19 = f32[16,2,4096]{2,1,0:T(2,128)} copy(f32[16,2,4096]{2,1,0:T(2,128)S(1)} %bitcast.34) | data formatting | bytes 1048576
Async XLA Ops:
  46.5 2.4 %copy-start = (f32[1024,128]{1,0:T(8,128)S(1)}, f32[1024,128]{1,0:T(8,128)}, u32[]{:S(2)}) copy-start(f32[1024,128]{1,0:T(8,128)} %get-tuple-element.5) | copy-start | bytes 1572868

commit v3 on v2

--- a/solution.py
+++ b/solution.py
@@ -129,6 +129,8 @@
     w_recv,
     modes,
     rotated,
+    wiener_rows,
+    picks,
     send_sem,
     recv_sem,
     load_sem,
@@ -149,6 +151,12 @@
         (ys[e] * NX + xs[d], {"blk": zl * PLANE + ys[e] * NX + xs[d]}) for e, d in PLANE_STEPS
     ]
     here = b % PLANE
+
+    barrier = pltpu.get_barrier_semaphore()
+    everyone = [p[-1] for p in plane_peers] + [p[-1] for p in z_peers]
+    everyone += [{"grp": other, **p[-1]} for p in z_peers] + [core_peer]
+    for peer in everyone:
+        pl.semaphore_signal(barrier, inc=1, device_id=peer, device_id_type=MESH)
 
     loads = [
         pltpu.make_async_copy(src, dst, load_sem.at[i])
@@ -167,10 +175,6 @@
     ]
     for load in loads:
         load.start()
-    barrier = pltpu.get_barrier_semaphore()
-    everyone = [core_peer] + [p[-1] for p in z_peers] + [p[-1] for p in plane_peers]
-    for peer in everyone:
-        pl.semaphore_signal(barrier, inc=1, device_id=peer, device_id_type=MESH)
 
     loads[0].wait()
     m = m_ref[...]
@@ -250,13 +254,21 @@
     for zl_, zh_, peer in z_peers:
         send(1, z_send.at[zl_], z_recv.at[2 * zl + zh], peer)
     keep(1, z_send.at[zl], z_recv.at[2 * zl + zh])
+    for h in range(2):
+        picks[h, :, :128] = order_rows(h)
     loads[7].wait()
     permute = cycle_order()
     for s in range(4):
         leg_p[s] = dot_nn(leg[s], permute).astype(BF16)
+    picks[2] = order_first()
+    picks[3] = order_last()
+    for h in range(2):
+        picks[4 + h, :128] = order_cols(h)
     arrived(1, z_recv)
     gathered = z_recv[...].reshape(256, 128)
-    turned = dot_nt(order_rows(0), gathered[:128]) + dot_nt(order_rows(1), gathered[128:])
+    turned = dot_nt(picks[0, :, :128], gathered[:128]) + dot_nt(
+        picks[1, :, :128], gathered[128:]
+    )
     p_send[...] = turned.astype(BF16).reshape(PLANE, 8, 128)
     slot = x * NY + y
     for i, peer in plane_peers:
@@ -266,7 +278,7 @@
     send(3, p_recv.at[g], p_recv.at[g], core_peer)
     arrived(3, p_recv.at[other])
 
-    first = order_first()
+    first = picks[2]
     columns = [
         dot_nn(first, p_recv[r].reshape(256, 128)).T for r in range(2)
     ]
@@ -283,16 +295,12 @@
             axis=1,
         ).astype(BF16)
         wiener = dot_nt(rows, leg_p[s]) * scale
-        for p in range(4):
-            for t in range(8):
-                wiener_out[pl.Slice((p // 2) * 1024 + (p % 2) * 32 + t * 4 + s, 16, 64), :] = wiener[
-                    16 * p : 16 * (p + 1), 128 * t : 128 * (t + 1)
-                ]
+        wiener_rows[s] = wiener
         partial = dot_nn(wiener.astype(BF16), leg_p[s]) * syn_scale
         back[0, s] = partial[:, :128]
         back[1, s] = partial[:, 128:]
-
-    send(4, back.at[other], back_buf, core_peer)
+        send(4, back.at[other, s], back_buf.at[s], core_peer)
+
     arrived(4, back_buf)
     both = back[g] + back_buf[...]
     halves = [
@@ -300,25 +308,34 @@
         for t in range(2)
     ]
     turned = jnp.concatenate(halves, axis=0).T.astype(BF16)
-    q_send[...] = dot_nn(order_last(), turned).astype(BF16).reshape(PLANE, 8, 128)
+    q_send[...] = dot_nn(picks[3], turned).astype(BF16).reshape(PLANE, 8, 128)
     for i, peer in plane_peers:
         send(5, q_send.at[i], q_recv.at[here], peer)
     keep(5, q_send.at[here], q_recv.at[here])
+    for s in range(4):
+        for p in range(4):
+            for t in range(8):
+                start = (p // 2) * 1024 + (p % 2) * 32 + t * 4 + s
+                wiener_out[pl.Slice(start, 16, 64), :] = wiener_rows[
+                    s, 16 * p : 16 * (p + 1), 128 * t : 128 * (t + 1)
+                ]
     arrived(5, q_recv)
     plane = q_recv[...].reshape(256, 128)
     for h in range(2):
-        turned = dot_nn(order_cols(h), plane).T.astype(BF16)
+        turned = dot_nn(picks[4 + h, :128], plane).T.astype(BF16)
         w_send[4 * h : 4 * h + 4] = turned.reshape(4, 32, 128)
+    mine = 2 * zl + zh
     for zl_, zh_, peer in z_peers:
-        send(6, w_send.at[2 * zl_ + zh_], w_recv.at[2 * zl + zh], peer)
-    keep(6, w_send.at[2 * zl + zh], w_recv.at[2 * zl + zh])
+        for core in (other, g):
+            send(6, w_send.at[2 * zl_ + zh_], w_recv.at[g, mine], {"grp": core, **peer})
+    send(6, w_send.at[mine], w_recv.at[g, mine], core_peer)
+    keep(6, w_send.at[mine], w_recv.at[g, mine])
     arrived(6, w_recv)
-    for t in range(NZL):
-        modes[g, :, 128 * t : 128 * (t + 1)] = (
-            w_recv[2 * t].astype(F32) + w_recv[2 * t + 1].astype(F32)
-        ).astype(BF16)
-    send(7, modes.at[g], modes.at[g], core_peer)
-    arrived(7, modes.at[other])
+    for r in range(2):
+        for t in range(NZL):
+            modes[r, :, 128 * t : 128 * (t + 1)] = (
+                w_recv[r, 2 * t].astype(F32) + w_recv[r, 2 * t + 1].astype(F32)
+            ).astype(BF16)
 
     for r in range(2):
         re, im = modes[r, :16].astype(F32), modes[r, 16:].astype(F32)
@@ -342,8 +359,38 @@
     left(3, p_recv.at[0])
     left(4, back_buf)
     left(5, q_recv.at[0:31])
-    left(6, w_recv.at[0:7])
-    left(7, modes.at[0])
+    left(6, w_recv.at[0])
+    left(6, w_recv.at[0, 0:7])
+
+
+def store_kernel(wiener, signal, wiener_out, signal_out, sem):
+    copies = []
+    for i, rows in enumerate([pl.ds(512 * n, 512) for n in range(4)]):
+        copies.append(pltpu.make_async_copy(wiener.at[rows], wiener_out.at[rows], sem.at[i]))
+        if i < 2:
+            copies.append(
+                pltpu.make_async_copy(signal.at[rows], signal_out.at[rows], sem.at[4 + i])
+            )
+    for copy in copies:
+        copy.start()
+    for copy in copies:
+        copy.wait()
+
+
+def store(wiener, signal):
+    hbm = pl.BlockSpec(memory_space=pltpu.HBM)
+    block = pl.BlockSpec(memory_space=pltpu.VMEM)
+    return pl.pallas_call(
+        store_kernel,
+        out_shape=(
+            jax.ShapeDtypeStruct((2048, 128), F32),
+            jax.ShapeDtypeStruct((1024, 128), F32),
+        ),
+        in_specs=[block] * 2,
+        out_specs=(hbm, hbm),
+        scratch_shapes=[pltpu.SemaphoreType.DMA((6,))],
+        compiler_params=pltpu.CompilerParams(vmem_limit_bytes=16 * 1024 * 1024),
+    )(wiener, signal)
 
 
 def step(inputs, syn_scale):
@@ -384,17 +431,19 @@
             vmem((PLANE, 8, 128)),
             vmem((PLANE, 8, 128)),
             vmem((NZ, 32, 128)),
-            vmem((NZ, 32, 128)),
+            vmem((2, NZ, 32, 128)),
             vmem((2, 32, ORDERS)),
             vmem((32 * BLOCKS, 2 * ORDERS)),
-            pltpu.SemaphoreType.DMA((8,)),
-            pltpu.SemaphoreType.DMA((8,)),
+            vmem((4, 64, 1024), F32),
+            vmem((6, 256, 256)),
+            pltpu.SemaphoreType.DMA((7,)),
+            pltpu.SemaphoreType.DMA((7,)),
             pltpu.SemaphoreType.DMA((8,)),
         ],
         compiler_params=pltpu.CompilerParams(
-            collective_id=0, has_side_effects=True, vmem_limit_bytes=67043328
+            collective_id=0, has_side_effects=True, vmem_limit_bytes=40000000
         ),
-    )(*inputs)
+    )(*[pltpu.with_memory_space_constraint(a, pltpu.HBM) for a in inputs])
 
 
 def per_device(
@@ -417,7 +466,7 @@
         spectrum[None],
         legendre,
     )
-    wiener, signal = step(inputs, syn_scale)
+    wiener, signal = store(*step(inputs, syn_scale))
     wiener_alm = (
         wiener.reshape(32, 2, 8, 4, 128).transpose(0, 1, 3, 2, 4).reshape(32, 2, 4, 1024)
     )

time: 49.8 us -> 44.9 us (0.902)
  local copies, waits for them, and re-layouts: 3.16 us -> 0 us
  Pallas kernels: 45.9 us -> 44.1 us
    unnamed x4 -> x0, local copies, waits for them, and re-layouts: 3.16 us -> none
    pallas_call x1, Pallas kernels: 45.9 us -> 43 us  [step(): pl.pallas_call(lambda *refs: step_kernel(syn_scale, *refs), out_shape=(ja...]
    pallas_call x0 -> x1, Pallas kernels: none -> 1.19 us  [store(): pl.pallas_call(store_kernel, out_shape=(jax.ShapeDtypeStruct((2048, 128),...]
where the time goes in v3:
time: 44.9 us; the launch traced here: 44.8 us
  Pallas kernels  44.1 us (98%)
  between operations  0.64 us (1%)
    pallas_call x1, Pallas kernels, step(): pl.pallas_call(lambda *refs: step_kernel(syn_scale, *refs), out_shape=(ja...  43 us
    pallas_call x1, Pallas kernels, store(): pl.pallas_call(store_kernel, out_shape=(jax.ShapeDtypeStruct((2048, 128),...  1.19 us

profile of v3, /device:TPU:1, one launch (start us, length us, event | category | flops | bytes accessed | tf_op | source)
XLA Modules:
  0.0 44.8 jit_solution(12850668596884375137)
XLA Ops:
  0.6 43.0 %shard_map.95 = (f32[2048,128]{1,0:T(8,128)S(1)}, f32[1024,128]{1,0:T(8,128)S(1)}) custom-call(f32[1024,128]{1,0:T(8,128)} %bitcast.33, f32[1024,128]{1,0:T(8,128)} %bitcast.34, f32[64,128]{1,0:T(8,128)} %bitcast.35, s32[64,128]{1,0:T(8,128)} %bitcast.36, s32[1,2]{1,0:T(1,128)} %bitcast.39, s32[1,512]{1,0:T(1,128)} %bitcast.38, f32[1,1024]{1,0:T(1,128)} %bitcast.37, ...), custom_call_target="tpu_custom_call" | custom-call | tf_op jit(solution)/shard_map/pallas_call | solution.py:401
  43.6 1.2 %shard_map.96 = (f32[2048,128]{1,0:T(8,128)}, f32[1024,128]{1,0:T(8,128)}) custom-call(f32[2048,128]{1,0:T(8,128)S(1)} %get-tuple-element.6.wiener, f32[1024,128]{1,0:T(8,128)S(1)} %get-tuple-element.7.signal), custom_call_target="tpu_custom_call" | custom-call | tf_op jit(solution)/shard_map/pallas_call | solution.py:383

commit v4 on v3

--- a/solution.py
+++ b/solution.py
@@ -116,7 +116,6 @@
     part,
     leg,
     leg_p,
-    core_buf,
     z_send,
     z_recv,
     p_send,
@@ -245,15 +244,17 @@
     def left(phase, ref):
         pltpu.make_async_copy(ref, ref, send_sem.at[phase]).wait()
 
-    send(0, part.at[other], core_buf, core_peer)
-    arrived(0, core_buf)
-    for c in range(2):
-        total = (part[g, c] + core_buf[c]).astype(BF16)
-        for t in range(NZL):
-            z_send[t, 16 * c : 16 * (c + 1)] = total[:, 128 * t : 128 * (t + 1)]
+    for r in range(2):
+        for c in range(2):
+            half = part[r, c].astype(BF16)
+            for t in range(NZL):
+                z_send[r, t, 16 * c : 16 * (c + 1)] = half[:, 128 * t : 128 * (t + 1)]
+    mine = 2 * zl + zh
     for zl_, zh_, peer in z_peers:
-        send(1, z_send.at[zl_], z_recv.at[2 * zl + zh], peer)
-    keep(1, z_send.at[zl], z_recv.at[2 * zl + zh])
+        for core in (other, g):
+            send(1, z_send.at[core, zl_], z_recv.at[g, mine], {"grp": core, **peer})
+    send(1, z_send.at[other, zl], z_recv.at[g, mine], core_peer)
+    keep(1, z_send.at[g, zl], z_recv.at[g, mine])
     for h in range(2):
         picks[h, :, :128] = order_rows(h)
     loads[7].wait()
@@ -265,7 +266,8 @@
     for h in range(2):
         picks[4 + h, :128] = order_cols(h)
     arrived(1, z_recv)
-    gathered = z_recv[...].reshape(256, 128)
+    gathered = z_recv[0].reshape(256, 128).astype(F32) + z_recv[1].reshape(256, 128).astype(F32)
+    gathered = gathered.astype(BF16)
     turned = dot_nt(picks[0, :, :128], gathered[:128]) + dot_nt(
         picks[1, :, :128], gathered[128:]
     )
@@ -324,7 +326,6 @@
     for h in range(2):
         turned = dot_nn(picks[4 + h, :128], plane).T.astype(BF16)
         w_send[4 * h : 4 * h + 4] = turned.reshape(4, 32, 128)
-    mine = 2 * zl + zh
     for zl_, zh_, peer in z_peers:
         for core in (other, g):
             send(6, w_send.at[2 * zl_ + zh_], w_recv.at[g, mine], {"grp": core, **peer})
@@ -353,8 +354,8 @@
                     16 * i : 16 * (i + 1), 128 * t : 128 * (t + 1)
                 ]
 
-    left(0, core_buf)
-    left(1, z_recv.at[0:7])
+    left(1, z_recv.at[0])
+    left(1, z_recv.at[0, 0:7])
     left(2, p_recv.at[0, 0:31])
     left(3, p_recv.at[0])
     left(4, back_buf)
@@ -421,9 +422,8 @@
             vmem((2, 2, 16, ORDERS), F32),
             vmem((4, 1024, 256)),
             vmem((4, 1024, 256)),
-            vmem((2, 16, ORDERS), F32),
-            vmem((NZL, 32, 128)),
-            vmem((NZ, 32, 128)),
+            vmem((2, NZL, 32, 128)),
+            vmem((2, NZ, 32, 128)),
             vmem((PLANE, 8, 128)),
             vmem((2, PLANE, 8, 128)),
             vmem((2, 4, 64, 128), F32),

time: 44.9 us -> 45 us (level)
  no operation moved by 1% of the time
where the time goes in v4:
time: 45 us; the launch traced here: 44.9 us
  Pallas kernels  44.3 us (98%)
  between operations  0.64 us (1%)
    pallas_call x1, Pallas kernels, step(): pl.pallas_call(lambda *refs: step_kernel(syn_scale, *refs), out_shape=(ja...  43.1 us
    pallas_call x1, Pallas kernels, store(): pl.pallas_call(store_kernel, out_shape=(jax.ShapeDtypeStruct((2048, 128),...  1.19 us

profile of v4, /device:TPU:1, one launch (start us, length us, event | category | flops | bytes accessed | tf_op | source)
XLA Modules:
  0.0 44.9 jit_solution(2548683108888948405)
XLA Ops:
  0.6 43.1 %shard_map.95 = (f32[2048,128]{1,0:T(8,128)S(1)}, f32[1024,128]{1,0:T(8,128)S(1)}) custom-call(f32[1024,128]{1,0:T(8,128)} %bitcast.33, f32[1024,128]{1,0:T(8,128)} %bitcast.34, f32[64,128]{1,0:T(8,128)} %bitcast.35, s32[64,128]{1,0:T(8,128)} %bitcast.36, s32[1,2]{1,0:T(1,128)} %bitcast.39, s32[1,512]{1,0:T(1,128)} %bitcast.38, f32[1,1024]{1,0:T(1,128)} %bitcast.37, ...), custom_call_target="tpu_custom_call" | custom-call | tf_op jit(solution)/shard_map/pallas_call | solution.py:402
  43.7 1.2 %shard_map.96 = (f32[2048,128]{1,0:T(8,128)}, f32[1024,128]{1,0:T(8,128)}) custom-call(f32[2048,128]{1,0:T(8,128)S(1)} %get-tuple-element.6.wiener, f32[1024,128]{1,0:T(8,128)S(1)} %get-tuple-element.7.signal), custom_call_target="tpu_custom_call" | custom-call | tf_op jit(solution)/shard_map/pallas_call | solution.py:384
